TPU v7x, 256 devices: a whole 4x4x8 slice. The times are simulated.
256 devices in a mesh: dp: 4 (over y_lo, core), tm: 4 (over x), rows: 16 (over z, y_hi).
Axes of the slice: x: 4, y: 4 (y_hi: 2, y_lo: 2; y = y_hi * 2 + y_lo), z: 8, core: 2. Of those that a mesh axis runs over, the one named last changes fastest.
Arguments:
- latents: bfloat16 [4, 8, 16, 30, 512], P('dp', 'tm', 'rows'), may hold values from -6 to 6
- grad_out: bfloat16 [4, 8, 32, 60, 256], P('dp', 'tm', 'rows'), may hold values from -6 to 6
- kernel: bfloat16 [3, 3, 3, 512, 256], replicated, may hold values from -0.0546875 to 0.0546875
Outputs:
- grad_latents: bfloat16 [4, 8, 16, 30, 512], P('dp', 'tm', 'rows')
- weight_grad: float32 [512, 3, 3, 3, 256], P(('dp', 'tm', 'rows'))
All inputs are finite; a program needn't handle non-finite values.
Results may differ from a plain program's by a relative error of at most 0.001.
Values may be sent and summed in bfloat16 or wider, within the bound.
A program may use at most 128 MiB of HBM per device.

v0:
```python
import jax
import jax.numpy as jnp
from jax import lax
from jax.sharding import PartitionSpec as P


def shift_from(shard, axis, by):
    peers = lax.axis_size(axis)
    pairs = [(i, i + by) for i in range(peers) if 0 <= i + by < peers]
    return lax.ppermute(shard, axis, pairs)


def pool_pairs(values, dim):
    n = values.shape[dim] // 2
    pad = [(0, 0)] * values.ndim
    pad[dim] = (1, 1)
    ext = jnp.pad(values, pad)
    out = []
    for i in range(3):
        start = 2 - i
        a = lax.slice_in_dim(ext, start, start + 2 * n - 1, stride=2, axis=dim)
        b = lax.slice_in_dim(ext, start + 1, start + 2 * n, stride=2, axis=dim)
        out.append(a + b)
    return jnp.stack(out, axis=dim + 1)


def body(latents, grad_out, kernel):
    frames = grad_out.shape[1]
    height = grad_out.shape[2]
    width = grad_out.shape[3]
    channels = latents.shape[4]
    outputs = grad_out.shape[4]
    devices = lax.axis_size("dp") * lax.axis_size("tm") * lax.axis_size("rows")
    factor = float(devices * frames * height * width) ** (-0.5)
    slab_count = lax.axis_size("rows")
    slab = lax.axis_index("rows")
    grad_whole = lax.all_gather(grad_out[0], "rows", axis=1, tiled=True)
    whole_height = grad_whole.shape[1]
    padded_rows = jnp.pad(grad_whole, ((0, 0), (1, 1), (0, 0), (0, 0)))
    near = lax.dynamic_slice_in_dim(padded_rows, slab * height, height + 2, axis=1)
    later = shift_from(near, "tm", -1)
    grad_all = jnp.concatenate([near, later], axis=0)
    grad_all = jnp.pad(grad_all, ((0, 0), (0, 0), (1, 1), (0, 0)))
    patches = []
    for a in range(3):
        for i in range(3):
            for j in range(3):
                patches.append(
                    grad_all[2 - a : 2 - a + frames, 2 - i : 2 - i + height, 2 - j : 2 - j + width]
                )
    patches = jnp.stack(patches, axis=3).reshape(frames * height * width, 27, outputs)
    grad_up = lax.dot_general(
        patches,
        kernel.reshape(27, channels, outputs),
        (((1, 2), (0, 2)), ((), ())),
        preferred_element_type=jnp.float32,
    )
    pooled = grad_up.reshape(frames, height // 2, 2, width // 2, 2, channels).sum(axis=(2, 4))
    grad_latents = pooled.astype(jnp.bfloat16)[None]
    groups = lax.axis_size("dp") * lax.axis_size("tm")
    share = channels // devices
    earlier = shift_from(latents, "tm", 1)
    with_earlier = jnp.concatenate([earlier, latents], axis=1)
    lead = with_earlier.shape[:4]
    regrouped = with_earlier.reshape(lead + (groups, slab_count, share))
    regrouped = jnp.swapaxes(regrouped, 4, 5).reshape(lead + (channels,))
    owned = lax.all_to_all(regrouped, "rows", split_axis=4, concat_axis=2, tiled=True)[0]
    group_channels = owned.shape[3]
    taps_a = jnp.stack([owned[a : a + frames] for a in range(3)], axis=0)
    pooled_grad = pool_pairs(pool_pairs(grad_whole.astype(jnp.float32), 1), 3)
    scaled = pooled_grad * 65537.0
    top = scaled - (scaled - pooled_grad)
    both = jnp.stack([top, pooled_grad - top], axis=0).astype(jnp.bfloat16)
    term = jnp.einsum("afrsc,xfrisjo->caijxo", taps_a, both, preferred_element_type=jnp.float32)
    term = (term[..., 0, :] + term[..., 1, :]) * factor
    term = term.reshape(group_channels, 3, 3, 3, outputs)
    term = lax.psum_scatter(term, "dp", scatter_dimension=0, tiled=True)
    weight_grad = lax.psum_scatter(term, "tm", scatter_dimension=0, tiled=True)
    return (grad_latents, weight_grad)


def solution(mesh):
    in_specs = (P("dp", "tm", "rows", None, None), P("dp", "tm", "rows", None, None), P())
    out_specs = (P("dp", "tm", "rows", None, None), P(("dp", "tm", "rows"), None, None, None, None))
    return jax.shard_map(body, mesh=mesh, in_specs=in_specs, out_specs=out_specs, check_vma=False)
```

profile of v0, /device:TPU:8, one launch (start us, length us, event | category | flops | bytes accessed | tf_op | source)
XLA Modules:
  0.0 254.9 jit_solution(13434810595302571663)
XLA Ops:
  7.2 1.6 copy.131
  8.8 3.4 %collective-permute-start.1 = (bf16[1,2,1,30,512]{4,1,3,2,0:T(2,128)(2,1)}, bf16[1,2,1,30,512]{4,1,3,2,0:T(2,128)(2,1)S(1)}, u32[]{:S(2)}, u32[]{:S(2)}) collective-permute-start(bf16[1,2,1,30,512]{4,1,3,2,0:T(2,128)(2,1)} %param.3), channel_id=1, source_target_pairs={{0,16},{16,32},{32,48},{1,17},{17,33},{33,49},{2,18},{18,34},{34,5... | collective-permute-start | bytes 184328 | tf_op jit(solution)/shard_map/ppermute | solution.py:10
  12.2 2.2 collective-permute-done.1
  14.4 1.0 pad_maximum_fusion.2
  16.5 1.6 reshape.331
  18.1 10.3 %all-to-all-start = ((bf16[16,2,1920]{2,1,0:T(2,128)(2,1)}), bf16[16,2,1920]{2,1,0:T(2,128)(2,1)S(1)}, u32[]{:S(2)}, u32[]{:S(2)}) async-start(bf16[16,2,1920]{2,1,0:T(2,128)(2,1)} %reshape.331), calls=%async_computation | async-start | bytes 245760 | tf_op jit(solution)/shard_map/all_to_all | solution.py:67
  29.7 10.4 %all-to-all-done = bf16[16,2,1920]{2,1,0:T(2,128)(2,1)S(1)} async-done(((bf16[16,2,1920]{2,1,0:T(2,128)(2,1)}), bf16[16,2,1920]{2,1,0:T(2,128)(2,1)S(1)}, u32[]{:S(2)}, u32[]{:S(2)}) %all-to-all-start) | async-done | bytes 122912 | tf_op jit(solution)/shard_map/all_to_all | solution.py:67
  40.1 1.4 reshape.332
  41.7 56.5 %all-gather.3.cloned.1.call-done = bf16[1,2,32,60,256]{4,3,2,1,0:T(8,128)(2,1)} async-done(((bf16[1,2,2,60,256]{4,3,2,1,0:T(8,128)(2,1)}), bf16[1,2,32,60,256]{4,3,2,1,0:T(8,128)(2,1)}) %all-gather.3.cloned.1.call-update) | async-done | bytes 1966096 | tf_op jit(solution)/shard_map/all_gather | solution.py:37
  98.2 1.1 pad_dynamic-slice_fusion.3
  100.4 1.0 add_bitcast_fusion.5
  101.5 3.3 %select_maximum_fusion = f32[2,16,3,62,256]{4,3,1,0,2:T(8,128)} fusion(f32[2,16,1,60,256]{4,3,1,0,2:T(8,128)S(1)} %get-tuple-element.14, f32[2,16,1,60,256]{4,3,1,0,2:T(8,128)S(1)} %get-tuple-element.13, f32[2,16,1,60,256]{4,3,1,0,2:T(8,128)S(1)} %get-tuple-element.12), kind=kLoop, calls=%fused_computation.11 | loop fusion | flops 12189696 | bytes 11993088 | tf_op jit(solution)/shard_map/stack | solution.py:24
  104.8 14.3 %slice.173 = f32[2,16,3,30,256]{4,3,1,0,2:T(8,128)} slice(f32[2,16,3,62,256]{4,3,1,0,2:T(8,128)} %select_maximum_fusion), slice={[0:2:1], [0:16:1], [0:3:1], [2:61:2], [0:256:1]} | slice | bytes 5898240 | tf_op jit(solution)/shard_map/slice | solution.py:21
  119.1 14.3 %slice.174 = f32[2,16,3,30,256]{4,3,1,0,2:T(8,128)} slice(f32[2,16,3,62,256]{4,3,1,0,2:T(8,128)} %select_maximum_fusion), slice={[0:2:1], [0:16:1], [0:3:1], [3:62:2], [0:256:1]} | slice | bytes 5898240 | tf_op jit(solution)/shard_map/slice | solution.py:22
  133.4 14.2 %slice.175 = f32[2,16,3,30,256]{4,3,1,0,2:T(8,128)} slice(f32[2,16,3,62,256]{4,3,1,0,2:T(8,128)} %select_maximum_fusion), slice={[0:2:1], [0:16:1], [0:3:1], [1:60:2], [0:256:1]} | slice | bytes 5898240 | tf_op jit(solution)/shard_map/slice | solution.py:21
  147.6 14.2 %slice.176 = f32[2,16,3,30,256]{4,3,1,0,2:T(8,128)} slice(f32[2,16,3,62,256]{4,3,1,0,2:T(8,128)} %select_maximum_fusion), slice={[0:2:1], [0:16:1], [0:3:1], [0:59:2], [0:256:1]} | slice | bytes 5898240 | tf_op jit(solution)/shard_map/slice | solution.py:21
  161.7 1.3 collective-permute-start
  163.6 7.2 %add_bitcast_fusion.2 = (f32[1,2,16,3,30,1,256]{6,4,2,1,5,3,0:T(8,128)S(1)}, f32[1,2,16,3,30,1,256]{6,4,2,1,5,3,0:T(8,128)S(1)}, f32[1,2,16,3,30,1,256]{6,4,2,1,5,3,0:T(8,128)S(1)}) fusion(f32[2,16,3,30,256]{4,3,1,0,2:T(8,128)} %slice.173, f32[2,16,3,30,256]{4,3,1,0,2:T(8,128)} %slice.174, f32[2,16,3,30,256]{4,3,1,0,2:T(8,128)} %slice.175, ...), kind=kLoop, calls=%fused_computation.18 | loop fusion | flops 2211840 | bytes 20643840 | tf_op jit(solution)/shard_map/stack | solution.py:24
  170.8 2.2 fusion.1
  173.0 1.7 fusion.9
  174.8 1.1 fusion.17
  176.8 0.7 copy_dynamic-update-slice_fusion.26
  181.3 0.7 copy_dynamic-update-slice_fusion.24
  183.4 0.7 copy_dynamic-update-slice_fusion.21
  189.4 0.7 copy_dynamic-update-slice_fusion.12
  191.4 0.7 copy_dynamic-update-slice_fusion.9
  193.5 0.7 copy_dynamic-update-slice_fusion.6
  194.2 0.7 copy_dynamic-update-slice_fusion.5
  198.2 6.1 %fusion.13 = bf16[2,30,512]{2,1,0:T(8,128)(2,1)S(1)} fusion(bf16[27,512,256,1,1,1]{2,1,0,5,4,3:T(8,128)(2,1)} %bitcast.141, bf16[2,1,2,30,2,27,256]{6,3,5,4,2,0,1:T(8,128)(2,1)} %copy_dynamic-update-slice_fusion), kind=kOutput, calls=%fused_computation.29 | convolution fusion | flops 1698785280 | bytes 10457088 | tf_op jit(solution)/shard_map/dot_general | solution.py:52
  204.4 0.7 copy.192
  205.1 41.7 %all-reduce.7.cloned.1.call-done = f32[8,3,3,3,256]{4,0,1,3,2:T(8,128)} async-done(((f32[8,3,3,3,256]{4,0,1,3,2:T(8,128)}), f32[8,3,3,3,256]{4,0,1,3,2:T(8,128)}) %all-reduce.7.cloned.1.call-update) | async-done | bytes 221200
  246.8 1.0 constant_dynamic-slice_fusion
  (72 shorter events, 21.6 us)
Async XLA Ops:
  7.2 21.3 %copy-start.1 = (u32[256]{0:T(256)S(1)}, u32[256]{0:T(256)}, u32[]{:S(2)}) copy-start(u32[256]{0:T(256)} %constant.32) | copy-start | bytes 3076
  7.2 91.0 %all-gather.3.cloned.1.call-start = ((), (), s32[]{:S(2)}) async-start(), calls=%async_computation.3 | async-start | bytes 2228224 | tf_op jit(solution)/shard_map/all_gather | solution.py:37
  8.8 5.6 %collective-permute-start.1 = (bf16[1,2,1,30,512]{4,1,3,2,0:T(2,128)(2,1)}, bf16[1,2,1,30,512]{4,1,3,2,0:T(2,128)(2,1)S(1)}, u32[]{:S(2)}, u32[]{:S(2)}) collective-permute-start(bf16[1,2,1,30,512]{4,1,3,2,0:T(2,128)(2,1)} %param.3), channel_id=1, source_target_pairs={{0,16},{16,32},{32,48},{1,17},{17,33},{33,49},{2,18},{18,34},{34,5... | collective-permute-start | bytes 184328 | tf_op jit(solution)/shard_map/ppermute | solution.py:10
  18.1 22.0 %all-to-all-start = ((bf16[16,2,1920]{2,1,0:T(2,128)(2,1)}), bf16[16,2,1920]{2,1,0:T(2,128)(2,1)S(1)}, u32[]{:S(2)}, u32[]{:S(2)}) async-start(bf16[16,2,1920]{2,1,0:T(2,128)(2,1)} %reshape.331), calls=%async_computation | async-start | bytes 245760 | tf_op jit(solution)/shard_map/all_to_all | solution.py:67
  28.4 169.8 %reduce-scatter.3.cloned.1.call-start = ((), (), s32[]{:S(2)}) async-start(), calls=%async_computation.2 | async-start | bytes 1105920 | tf_op jit(solution)/shard_map/reduce_scatter | solution.py:77
  98.2 1.7 copy-start
  161.7 14.3 %collective-permute-start = (bf16[2,4,60,256]{3,2,1,0:T(8,128)(2,1)S(1)}, bf16[2,4,60,256]{3,2,1,0:T(8,128)(2,1)S(1)}, u32[]{:S(2)}, u32[]{:S(2)}) collective-permute-start(bf16[2,4,60,256]{3,2,1,0:T(8,128)(2,1)S(1)} %pad_dynamic-slice_fusion.3), channel_id=1, source_target_pairs={{16,0},{32,16},{48,32},{17,1},{33,17},{49,33},{18,2},{34,18},{50,3... | collective-permute-start | bytes 737288 | tf_op jit(solution)/shard_map/ppermute | solution.py:10
  175.9 70.9 %all-reduce.7.cloned.1.call-start = ((), (), s32[]{:S(2)}) async-start(), calls=%async_computation.4 | async-start | bytes 442368
Sparse Core Ops, SparseCore 0:
  10.6 87.5 all-gather.2
  176.0 19.1 reduce-scatter.2
  198.4 48.3 all-reduce.6
where the time goes:
time: 257 us; the launch traced here: 255 us
  waiting for transfers between devices  111 us (43%)
  local copies, waits for them, and re-layouts  89.7 us (35%)
  other arithmetic  16.5 us (6%)
  starting transfers between devices  15.3 us (6%)
  between operations  14.8 us (6%)
  matrix products  7.84 us (3%)
    all_gather x1, waiting for transfers between devices, body(): grad_whole = lax.all_gather(grad_out[0], 'rows', axis=1, tiled=True)  56.5 us
    slice x3, local copies, waits for them, and re-layouts, pool_pairs(): a = lax.slice_in_dim(ext, start, start + 2 * n - 1, stride=2, axis=dim)  42.7 us
    unnamed x4, waiting for transfers between devices  41.8 us
    unnamed x37, local copies, waits for them, and re-layouts  25.6 us
    slice x1, local copies, waits for them, and re-layouts, pool_pairs(): b = lax.slice_in_dim(ext, start + 1, start + 2 * n, stride=2, axis=dim)  14.3 us
    another operation x3, other arithmetic, pool_pairs(): return jnp.stack(out, axis=dim + 1)  11.5 us
    all_to_all x1, waiting for transfers between devices, body(): lax.all_to_all(regrouped, 'rows', split_axis=4, concat_axis=2, tiled=True)  10.4 us
    all_to_all x1, starting transfers between devices, body(): lax.all_to_all(regrouped, 'rows', split_axis=4, concat_axis=2, tiled=True)  10.3 us
  transfers between devices with their start and end apart: 6, of which 4 were waited for; matrix products, arithmetic and copies ran while one was open for 19% of the time, Pallas kernels for 0%

commit v1 on v0

--- a/solution.py
+++ b/solution.py
@@ -34,7 +34,10 @@
     factor = float(devices * frames * height * width) ** (-0.5)
     slab_count = lax.axis_size("rows")
     slab = lax.axis_index("rows")
-    grad_whole = lax.all_gather(grad_out[0], "rows", axis=1, tiled=True)
+    local_x = grad_out[0]
+    grad_whole = jnp.concatenate(
+        jax.lax.all_to_all(jnp.stack(jax.lax.axis_size("rows") * [local_x], 0), "rows", 0, 0), 1
+    )
     whole_height = grad_whole.shape[1]
     padded_rows = jnp.pad(grad_whole, ((0, 0), (1, 1), (0, 0), (0, 0)))
     near = lax.dynamic_slice_in_dim(padded_rows, slab * height, height + 2, axis=1)

time: 257 us -> 250 us (0.973)
  waiting for transfers between devices: 111 us -> 87.3 us
  blocking collectives: 0 us -> 21.2 us
  starting transfers between devices: 15.3 us -> 8.79 us
    all_gather x1 -> x0, waiting for transfers between devices: 56.5 us -> none  [body(): grad_whole = lax.all_gather(grad_out[0], 'rows', axis=1, tiled=True)]
    all_to_all x1, waiting for transfers between devices: 10.4 us -> 44.5 us  [body(): jax.lax.all_to_all(jnp.stack(jax.lax.axis_size('rows') * [local_x], 0), '...]
    all_to_all x0 -> x1, blocking collectives: none -> 21.2 us  [body(): lax.all_to_all(regrouped, 'rows', split_axis=4, concat_axis=2, tiled=True)]
    all_to_all x1, starting transfers between devices: 10.3 us -> 3.72 us  [body(): jax.lax.all_to_all(jnp.stack(jax.lax.axis_size('rows') * [local_x], 0), '...]
    unnamed x37 -> x38, local copies, waits for them, and re-layouts: 25.6 us -> 24 us
    unnamed x4 -> x3, waiting for transfers between devices: 41.8 us -> 40.6 us
  transfers between devices with their start and end apart: 6 -> 5, of which waited for: 4 -> 3; matrix products, arithmetic and copies ran while one was open for 19% -> 18% of each run, Pallas kernels for 0% -> 0%
where the time goes in v1:
time: 250 us; the launch traced here: 248 us
  local copies, waits for them, and re-layouts  91.3 us (37%)
  waiting for transfers between devices  87.3 us (35%)
  blocking collectives  21.2 us (8%)
  other arithmetic  16.5 us (7%)
  between operations  15.1 us (6%)
  starting transfers between devices  8.79 us (4%)
  matrix products  7.84 us (3%)
    all_to_all x1, waiting for transfers between devices, body(): jax.lax.all_to_all(jnp.stack(jax.lax.axis_size('rows') * [local_x], 0), '...  44.5 us
    slice x3, local copies, waits for them, and re-layouts, pool_pairs(): a = lax.slice_in_dim(ext, start, start + 2 * n - 1, stride=2, axis=dim)  42.7 us
    unnamed x3, waiting for transfers between devices  40.6 us
    unnamed x38, local copies, waits for them, and re-layouts  24 us
    all_to_all x1, blocking collectives, body(): lax.all_to_all(regrouped, 'rows', split_axis=4, concat_axis=2, tiled=True)  21.2 us
    slice x1, local copies, waits for them, and re-layouts, pool_pairs(): b = lax.slice_in_dim(ext, start + 1, start + 2 * n, stride=2, axis=dim)  14.3 us
    another operation x3, other arithmetic, pool_pairs(): return jnp.stack(out, axis=dim + 1)  11.5 us
    dot_general x1, matrix products, body(): lax.dot_general(patches, kernel.reshape(27, channels, outputs), (((1, 2),...  6.12 us
  transfers between devices with their start and end apart: 5, of which 3 were waited for; matrix products, arithmetic and copies ran while one was open for 18% of the time, Pallas kernels for 0%

profile of v1, /device:TPU:8, one launch (start us, length us, event | category | flops | bytes accessed | tf_op | source)
XLA Modules:
  0.0 248.0 jit_solution(839780133481830368)
XLA Ops:
  7.2 3.5 %collective-permute-start.1 = (bf16[1,2,1,30,512]{4,1,3,2,0:T(2,128)(2,1)}, bf16[1,2,1,30,512]{4,1,3,2,0:T(2,128)(2,1)S(1)}, u32[]{:S(2)}, u32[]{:S(2)}) collective-permute-start(bf16[1,2,1,30,512]{4,1,3,2,0:T(2,128)(2,1)} %param.3), channel_id=1, source_target_pairs={{0,16},{16,32},{32,48},{1,17},{17,33},{33,49},{2,18},{18,34},{34,5... | collective-permute-start | bytes 184328 | tf_op jit(solution)/shard_map/ppermute | solution.py:10
  10.7 2.2 collective-permute-done.1
  12.9 1.0 pad_maximum_fusion.2
  15.0 1.0 reshape.339
  15.9 21.2 %all_to_all.20 = bf16[16,2,1920]{2,1,0:T(2,128)(2,1)S(1)} all-to-all(bf16[16,2,1920]{2,1,0:T(2,128)(2,1)S(1)} %reshape.339), channel_id=1, replica_groups=mesh['dp'=4,'tm'=4,'rows'=16] {'rows'}, dimensions={0} | all-to-all | bytes 245760 | tf_op jit(solution)/shard_map/all_to_all | solution.py:70
  37.1 2.3 stack.129
  39.4 3.7 %all-to-all-start = ((bf16[16,2,2,60,256]{4,2,3,1,0:T(2,128)(2,1)}), bf16[16,2,2,60,256]{4,2,3,1,0:T(2,128)(2,1)S(1)}, u32[]{:S(2)}, u32[]{:S(2)}) async-start(bf16[16,2,2,60,256]{4,2,3,1,0:T(2,128)(2,1)} %stack.129), calls=%async_computation | async-start | bytes 3932160 | tf_op jit(solution)/shard_map/all_to_all | solution.py:39
  44.4 1.4 reshape.340
  46.0 44.5 %all-to-all-done = bf16[16,2,2,60,256]{4,2,3,1,0:T(2,128)(2,1)S(1)} async-done(((bf16[16,2,2,60,256]{4,2,3,1,0:T(2,128)(2,1)}), bf16[16,2,2,60,256]{4,2,3,1,0:T(2,128)(2,1)S(1)}, u32[]{:S(2)}, u32[]{:S(2)}) %all-to-all-start) | async-done | bytes 1966112 | tf_op jit(solution)/shard_map/all_to_all | solution.py:39
  90.5 1.3 copy-done
  91.8 1.9 copy.131
  94.4 1.0 add_bitcast_fusion.5
  95.4 3.3 %select_maximum_fusion = f32[2,16,3,62,256]{4,3,1,0,2:T(8,128)} fusion(f32[2,16,1,60,256]{4,3,1,0,2:T(8,128)S(1)} %get-tuple-element.14, f32[2,16,1,60,256]{4,3,1,0,2:T(8,128)S(1)} %get-tuple-element.13, f32[2,16,1,60,256]{4,3,1,0,2:T(8,128)S(1)} %get-tuple-element.12), kind=kLoop, calls=%fused_computation.11 | loop fusion | flops 12189696 | bytes 11993088 | tf_op jit(solution)/shard_map/stack | solution.py:24
  98.7 14.3 %slice.173 = f32[2,16,3,30,256]{4,3,1,0,2:T(8,128)} slice(f32[2,16,3,62,256]{4,3,1,0,2:T(8,128)} %select_maximum_fusion), slice={[0:2:1], [0:16:1], [0:3:1], [2:61:2], [0:256:1]} | slice | bytes 5898240 | tf_op jit(solution)/shard_map/slice | solution.py:21
  113.0 14.3 %slice.174 = f32[2,16,3,30,256]{4,3,1,0,2:T(8,128)} slice(f32[2,16,3,62,256]{4,3,1,0,2:T(8,128)} %select_maximum_fusion), slice={[0:2:1], [0:16:1], [0:3:1], [3:62:2], [0:256:1]} | slice | bytes 5898240 | tf_op jit(solution)/shard_map/slice | solution.py:22
  127.3 14.2 %slice.175 = f32[2,16,3,30,256]{4,3,1,0,2:T(8,128)} slice(f32[2,16,3,62,256]{4,3,1,0,2:T(8,128)} %select_maximum_fusion), slice={[0:2:1], [0:16:1], [0:3:1], [1:60:2], [0:256:1]} | slice | bytes 5898240 | tf_op jit(solution)/shard_map/slice | solution.py:21
  141.4 14.2 %slice.176 = f32[2,16,3,30,256]{4,3,1,0,2:T(8,128)} slice(f32[2,16,3,62,256]{4,3,1,0,2:T(8,128)} %select_maximum_fusion), slice={[0:2:1], [0:16:1], [0:3:1], [0:59:2], [0:256:1]} | slice | bytes 5898240 | tf_op jit(solution)/shard_map/slice | solution.py:21
  155.6 1.3 collective-permute-start
  157.4 7.2 %add_bitcast_fusion.2 = (f32[1,2,16,3,30,1,256]{6,4,2,1,5,3,0:T(8,128)S(1)}, f32[1,2,16,3,30,1,256]{6,4,2,1,5,3,0:T(8,128)S(1)}, f32[1,2,16,3,30,1,256]{6,4,2,1,5,3,0:T(8,128)S(1)}) fusion(f32[2,16,3,30,256]{4,3,1,0,2:T(8,128)} %slice.173, f32[2,16,3,30,256]{4,3,1,0,2:T(8,128)} %slice.174, f32[2,16,3,30,256]{4,3,1,0,2:T(8,128)} %slice.175, ...), kind=kLoop, calls=%fused_computation.18 | loop fusion | flops 2211840 | bytes 20643840 | tf_op jit(solution)/shard_map/stack | solution.py:24
  164.7 2.2 fusion.1
  166.9 1.7 fusion.9
  168.6 1.1 fusion.17
  170.7 0.7 copy_dynamic-update-slice_fusion.26
  174.6 0.7 copy_dynamic-update-slice_fusion.25
  176.6 0.7 copy_dynamic-update-slice_fusion.22
  178.6 0.7 copy_dynamic-update-slice_fusion.19
  188.7 0.7 copy_dynamic-update-slice_fusion.4
  189.4 0.7 copy_dynamic-update-slice_fusion.3
  192.2 6.1 %fusion.13 = bf16[2,30,512]{2,1,0:T(8,128)(2,1)S(1)} fusion(bf16[27,512,256,1,1,1]{2,1,0,5,4,3:T(8,128)(2,1)} %bitcast.145, bf16[2,1,2,30,2,27,256]{6,3,5,4,2,0,1:T(8,128)(2,1)} %copy_dynamic-update-slice_fusion), kind=kOutput, calls=%fused_computation.29 | convolution fusion | flops 1698785280 | bytes 10457088 | tf_op jit(solution)/shard_map/dot_general | solution.py:55
  198.3 0.7 copy.192
  199.0 40.6 %all-reduce.7.cloned.1.call-done = f32[8,3,3,3,256]{4,0,1,3,2:T(8,128)} async-done(((f32[8,3,3,3,256]{4,0,1,3,2:T(8,128)}), f32[8,3,3,3,256]{4,0,1,3,2:T(8,128)}) %all-reduce.7.cloned.1.call-update) | async-done | bytes 221200
  239.6 1.0 constant_dynamic-slice_fusion
  (73 shorter events, 21.7 us)
Async XLA Ops:
  7.2 29.9 %copy-start.1 = (bf16[1,2,2,60,256]{4,2,3,1,0:T(2,128)(2,1)S(1)}, bf16[1,2,2,60,256]{4,2,3,1,0:T(2,128)(2,1)}, u32[]{:S(2)}) copy-start(bf16[1,2,2,60,256]{4,2,3,1,0:T(2,128)(2,1)} %param.4) | copy-start | bytes 368644
  7.2 5.7 %collective-permute-start.1 = (bf16[1,2,1,30,512]{4,1,3,2,0:T(2,128)(2,1)}, bf16[1,2,1,30,512]{4,1,3,2,0:T(2,128)(2,1)S(1)}, u32[]{:S(2)}, u32[]{:S(2)}) collective-permute-start(bf16[1,2,1,30,512]{4,1,3,2,0:T(2,128)(2,1)} %param.3), channel_id=1, source_target_pairs={{0,16},{16,32},{32,48},{1,17},{17,33},{33,49},{2,18},{18,34},{34,5... | collective-permute-start | bytes 184328 | tf_op jit(solution)/shard_map/ppermute | solution.py:10
  15.0 28.2 %copy-start.2 = (u32[256]{0:T(256)S(1)}, u32[256]{0:T(256)}, u32[]{:S(2)}) copy-start(u32[256]{0:T(256)} %constant.32) | copy-start | bytes 3076
  39.4 51.1 %all-to-all-start = ((bf16[16,2,2,60,256]{4,2,3,1,0:T(2,128)(2,1)}), bf16[16,2,2,60,256]{4,2,3,1,0:T(2,128)(2,1)S(1)}, u32[]{:S(2)}, u32[]{:S(2)}) async-start(bf16[16,2,2,60,256]{4,2,3,1,0:T(2,128)(2,1)} %stack.129), calls=%async_computation | async-start | bytes 3932160 | tf_op jit(solution)/shard_map/all_to_all | solution.py:39
  43.1 149.0 %reduce-scatter.3.cloned.1.call-start = ((), (), s32[]{:S(2)}) async-start(), calls=%async_computation.3 | async-start | bytes 1105920 | tf_op jit(solution)/shard_map/reduce_scatter | solution.py:80
  90.5 1.3 copy-start
  155.6 14.3 %collective-permute-start = (bf16[2,4,60,256]{3,2,1,0:T(8,128)(2,1)S(1)}, bf16[2,4,60,256]{3,2,1,0:T(8,128)(2,1)S(1)}, u32[]{:S(2)}, u32[]{:S(2)}) collective-permute-start(bf16[2,4,60,256]{3,2,1,0:T(8,128)(2,1)S(1)} %pad_dynamic-slice_fusion.3), channel_id=1, source_target_pairs={{16,0},{32,16},{48,32},{17,1},{33,17},{49,33},{18,2},{34,18},{50,3... | collective-permute-start | bytes 737288 | tf_op jit(solution)/shard_map/ppermute | solution.py:10
  169.7 69.8 %all-reduce.7.cloned.1.call-start = ((), (), s32[]{:S(2)}) async-start(), calls=%async_computation.4 | async-start | bytes 442368
Sparse Core Ops, SparseCore 0:
  169.9 18.0 reduce-scatter.2
  192.3 47.2 all-reduce.6
